TPU v7x, 256 devices: a whole 4x4x8 slice. The times are simulated.
256 devices in a mesh: seq: 64 (over x, z, core), head: 4 (over y).
Axes of the slice: x: 4, y: 4, z: 8, core: 2. Of those that a mesh axis runs over, the one named last changes fastest.
Arguments:
- values: float32 [16384, 2560], P('seq', 'head'), may hold values from -6 to 6
- input_map: float32 [16384, 128], P('seq'), may hold values from -6 to 6
- output_map: float32 [16384, 128], P('seq'), may hold values from -6 to 6
- step_sizes: float32 [40, 16384], P('head', 'seq'), may hold values from 0.004 to 0.02
- decay_rates: float32 [40], P('head'), may hold values from 0.02 to 2
- skip_gains: float32 [40], P('head'), may hold values from 0.5 to 1.5
- doc_lengths: int32 [128], replicated, may hold values from 1 to 1024, 16384 in all
- out_grad: float32 [16384, 2560], P('seq', 'head'), may hold values from -6 to 6
Outputs:
- outputs: bfloat16 [16384, 2560], P('seq', 'head')
- grad_values: bfloat16 [16384, 2560], P('seq', 'head')
- grad_input_map: float32 [16384, 128], P('seq')
- grad_output_map: float32 [16384, 128], P('seq')
Inputs may be any that keep to these rules, and one draw needn't show every extreme that they name: `doc_lengths`: the documents fill the stream of 16384 tokens in order; no document has more than 1024 tokens, and one has exactly that many.
All inputs are finite; a program needn't handle non-finite values.
Results may differ from a plain program's by a relative error of at most 0.001.
Values sent between devices are 32-bit elements; how exact they have to be, the bound alone decides.
No kernel may reach another device: no remote copies, remote signals or barrier semaphores. Data moves between devices by JAX's collectives and lax.ppermute only.
A program may use at most 128 MiB of HBM per device.

v0:
```python
import jax
import jax.numpy as jnp
from jax import lax
from jax.sharding import PartitionSpec as P

HEAD_SIZE = 64
GROUP = 256


highest = lax.Precision.HIGHEST


def entering_2(part, axis, combine, identity, reverse):
    count = lax.axis_size(axis)
    place = lax.axis_index(axis)
    ahead = count - 1 - place if reverse else place
    gathered = jax.tree.map(lambda a: lax.all_gather(a, axis), part)
    state = jax.tree.map(lambda a, e: jnp.zeros_like(a) + jnp.asarray(e, a.dtype), part, identity)

    def one(hop, state):
        source = count - 1 - hop if reverse else hop
        return combine(
            state, jax.tree.map(lambda a: lax.dynamic_index_in_dim(a, source, 0, False), gathered)
        )

    return lax.fori_loop(0, ahead, one, state)


def edge_decays(log_decay, restart):
    running = jnp.cumsum(log_decay, axis=1)
    resets_seen = jnp.cumsum(restart)
    inward = jnp.where(resets_seen[None, :] == 0, jnp.exp(running), 0.0)
    outward = jnp.where(
        resets_seen[None, :] == resets_seen[-1], jnp.exp(running[:, -1:] - running), 0.0
    )
    whole_decay = jnp.where(resets_seen[-1] == 0, jnp.exp(running[:, -1]), 0.0)
    return (running, resets_seen, inward, outward, whole_decay)


def group_pass(values, bmat, cmat, steps, rates, skips, restart, grad_y):
    length, head_count, head_width = values.shape
    blocks = length // GROUP
    log_decay = -rates[:, None] * steps

    def blocked(array):
        return array.reshape((blocks, GROUP) + array.shape[1:])

    def blocked_heads(array):
        return jnp.transpose(array.reshape(head_count, blocks, GROUP), (1, 0, 2))

    grouped = (
        blocked(values),
        blocked(grad_y),
        blocked(bmat),
        blocked(cmat),
        blocked_heads(steps),
        blocked_heads(log_decay),
        blocked(restart),
    )
    causal = jnp.arange(GROUP)[:, None] >= jnp.arange(GROUP)[None, :]

    def forward(carry_state, item):
        piece_x, piece_g, piece_b, piece_c, piece_dt, piece_log, piece_reset = item
        running, resets_seen, inward, outward, whole_decay = edge_decays(piece_log, piece_reset)
        visible = causal & (resets_seen[:, None] == resets_seen[None, :])
        inner = jnp.where(
            visible[None], jnp.exp(jnp.minimum(running[:, :, None] - running[:, None, :], 0.0)), 0.0
        )
        scaled = piece_x * piece_dt.T[:, :, None]
        scores = jnp.dot(piece_c, piece_b.T, precision=highest)
        mixing = inner * scores[None]
        entering = inward.T[:, :, None]
        result = jnp.einsum("hts,shp->thp", mixing, scaled, precision=highest)
        result = result + entering * jnp.einsum(
            "tn,hpn->thp", piece_c, carry_state, precision=highest
        )
        result = result + skips[None, :, None] * piece_x
        products = jnp.einsum("thp,shp->hts", piece_g, piece_x, precision=highest)
        weight = inner * products * piece_dt[:, None, :]
        grad_x = (
            jnp.einsum("hts,thp->shp", mixing, piece_g, precision=highest) * piece_dt.T[:, :, None]
        )
        grad_x = grad_x + skips[None, :, None] * piece_g
        grad_b = jnp.einsum("hts,tn->sn", weight, piece_c, precision=highest)
        grad_c = jnp.einsum("hts,sn->tn", weight, piece_b, precision=highest)
        grad_c = grad_c + jnp.einsum(
            "hpn,thp->tn", carry_state, piece_g * entering, precision=highest
        )
        updated = whole_decay[:, None, None] * carry_state + jnp.einsum(
            "shp,sn->hpn", scaled * outward.T[:, :, None], piece_b, precision=highest
        )
        return (updated, (result, grad_x, grad_b, grad_c, inward, outward, whole_decay))

    zeros_state = jnp.zeros((head_count, head_width, bmat.shape[1]), jnp.float32)
    end_state, outs = lax.scan(forward, zeros_state, grouped)
    result, grad_x, grad_b, grad_c, inwards, outwards, wholes = outs

    def backward(carry_grad, item):
        piece_x, piece_g, piece_b, piece_c, piece_dt, inward, outward, whole_decay = item
        factor = (piece_dt * outward).T[:, :, None]
        extra_x = factor * jnp.einsum("hpn,sn->shp", carry_grad, piece_b, precision=highest)
        extra_b = jnp.einsum("hpn,shp->sn", carry_grad, piece_x * factor, precision=highest)
        earlier_grad = whole_decay[:, None, None] * carry_grad + jnp.einsum(
            "thp,tn->hpn", piece_g * inward.T[:, :, None], piece_c, precision=highest
        )
        return (earlier_grad, (extra_x, extra_b))

    start_grad, (extra_x, extra_b) = lax.scan(
        backward,
        zeros_state,
        (grouped[0], grouped[1], grouped[2], grouped[3], grouped[4], inwards, outwards, wholes),
        reverse=True,
    )
    result = result.reshape(length, head_count, head_width)
    grad_x = (grad_x + extra_x).reshape(length, head_count, head_width)
    grad_b = (grad_b + extra_b).reshape(length, -1)
    grad_c = grad_c.reshape(length, -1)
    return (result, grad_x, grad_b, grad_c, end_state, start_grad)


def combine_pair(earlier, later_part):
    return (earlier[0] * later_part[0], later_part[0][:, None, None] * earlier[1] + later_part[1])


def body(values, input_map, output_map, step_sizes, decay_rates, skip_gains, doc_lengths, out_grad):
    length = values.shape[0]
    head_count = values.shape[1] // HEAD_SIZE
    shaped_x = values.reshape(length, head_count, HEAD_SIZE)
    shaped_g = out_grad.reshape(length, head_count, HEAD_SIZE)
    positions = lax.axis_index("seq") * length + jnp.arange(length, dtype=jnp.int32)
    starts = jnp.cumsum(doc_lengths) - doc_lengths
    restart = jnp.any(starts[:, None] == positions[None, :], axis=0).astype(jnp.float32)
    result, grad_x, grad_b, grad_c, end_state, start_grad = group_pass(
        shaped_x, input_map, output_map, step_sizes, decay_rates, skip_gains, restart, shaped_g
    )
    running, resets_seen, inward, outward, whole_decay = edge_decays(
        -decay_rates[:, None] * step_sizes, restart
    )
    identity = (jnp.ones_like(whole_decay), jnp.zeros_like(end_state))
    state_in = entering_2((whole_decay, end_state), "seq", combine_pair, identity, False)[1]
    grad_after = entering_2((whole_decay, start_grad), "seq", combine_pair, identity, True)[1]
    entering = inward.T[:, :, None]
    result = result + entering * jnp.einsum("tn,hpn->thp", output_map, state_in, precision=highest)
    grad_c = grad_c + jnp.einsum("hpn,thp->tn", state_in, shaped_g * entering, precision=highest)
    factor = (step_sizes * outward).T[:, :, None]
    grad_x = grad_x + factor * jnp.einsum("hpn,sn->shp", grad_after, input_map, precision=highest)
    grad_b = grad_b + jnp.einsum("hpn,shp->sn", grad_after, shaped_x * factor, precision=highest)
    grad_b, grad_c = lax.psum((grad_b, grad_c), "head")
    return (
        result.reshape(length, -1).astype(jnp.bfloat16),
        grad_x.reshape(length, -1).astype(jnp.bfloat16),
        grad_b,
        grad_c,
    )


def solution(mesh):
    placed = (
        P("seq", "head"),
        P("seq", None),
        P("seq", None),
        P("head", "seq"),
        P("head"),
        P("head"),
        P(),
        P("seq", "head"),
    )
    return jax.shard_map(
        body,
        mesh=mesh,
        in_specs=placed,
        out_specs=(P("seq", "head"), P("seq", "head"), P("seq", None), P("seq", None)),
        check_vma=False,
    )
```

profile of v0, /device:TPU:2, one launch (start us, length us, event | category | flops | bytes accessed | tf_op | source)
XLA Modules:
  0.0 414.2 jit_solution(13744933926897372859)
XLA Ops:
  14.2 1.3 copy.36
  16.4 2.3 convolution_add_fusion.1
  19.2 1.4 convolution_add_fusion
  22.2 113.7 %all-reduce = f32[640]{0:T(1024)S(1)} all-reduce(f32[640]{0:T(1024)S(1)} %dynamic-update-slice), channel_id=2, replica_groups=mesh['seq'=64,'head'=4] {'seq'}, use_global_device_ids=true, to_apply=%add | all-reduce | flops 640 | bytes 5120
  136.6 1.9 convolution_bitcast_fusion.7
  138.5 1.9 convolution_bitcast_fusion.5
  141.6 2.5 fusion.27
  144.8 3.0 multiply_reduce_fusion
  147.9 29.0 %while.16 = (s32[]{:T(128)}, f32[10,64,128]{2,1,0:T(8,128)S(1)}, s32[]{:T(128)}, f32[64,10]{1,0:T(8,128)}, f32[64,10,64,128]{3,2,1,0:T(8,128)}, /*index=5*/s32[]{:T(128)}, s32[]{:T(128)}, s32[]{:T(128)}) while((s32[]{:T(128)}, f32[10,64,128]{2,1,0:T(8,128)S(1)}, s32[]{:T(128)}, f32[64,10]{1,0:T(8,128)}, f32[64,10,64,128]{3,2,1,0:T(8,128)}, ...), condition=%wide.region_7.8_spmd, body=%wide.region_6.7_spmd.sunk | while | flops 163845 | bytes 983287 | solution.py:26
  150.4 1.1 bitcast_add_fusion.4
  159.5 1.1 bitcast_add_fusion.4
  163.1 1.1 bitcast_add_fusion.4
  164.9 1.1 bitcast_add_fusion.4
  170.3 1.1 bitcast_add_fusion.4
  175.8 1.1 bitcast_add_fusion.4
  176.9 1.9 convolution_bitcast_fusion.4
  178.8 1.5 fusion.40
  180.3 61.0 %all-gather.8.cloned.1.call-done = f32[640,64,128]{2,1,0:T(8,128)} async-done(((f32[10,64,128]{2,1,0:T(8,128)}), f32[640,64,128]{2,1,0:T(8,128)}) %all-gather.8.cloned.1.call-update) | async-done | bytes 20971536 | tf_op jit(solution)/shard_map/all_gather | solution.py:17
  241.3 85.4 %while.17 = (s32[]{:T(128)}, f32[10,64,128]{2,1,0:T(8,128)S(1)}, s32[]{:T(128)}, f32[64,10]{1,0:T(8,128)}, f32[64,10,64,128]{3,2,1,0:T(8,128)}, /*index=5*/s32[]{:T(128)}, s32[]{:T(128)}, s32[]{:T(128)}, s32[]{:T(128)}) while((s32[]{:T(128)}, f32[10,64,128]{2,1,0:T(8,128)S(1)}, s32[]{:T(128)}, f32[64,10]{1,0:T(8,128)}, ...), condition=%wide.region_9.10_spmd, body=%wide.region_8.9_spmd.sunk | while | flops 163846 | bytes 983307 | solution.py:26
  265.6 1.1 bitcast_add_fusion.5
  267.4 1.1 bitcast_add_fusion.5
  269.2 1.1 bitcast_add_fusion.5
  271.0 1.1 bitcast_add_fusion.5
  300.0 1.1 bitcast_add_fusion.5
  301.8 1.1 bitcast_add_fusion.5
  303.6 1.1 bitcast_add_fusion.5
  326.7 1.9 convolution_bitcast_fusion.6
  330.2 2.2 fusion.47
  333.4 4.3 %fusion.43 = bf16[256,10,64]{0,2,1:T(8,128)(2,1)S(1)} fusion(f32[256,10,64]{0,2,1:T(8,128)} %fusion.40, f32[256,10,64]{0,2,1:T(8,128)S(1)} %fusion.41, f32[256,256]{1,0:T(8,128)} %copy-done.6, f32[10,256]{1,0:T(8,128)} %bitcast.138, pred[256,256]{1,0:T(8,128)(4,1)} %copy-done.9, f32[256,10,64]{0,2,1:T(8,128)S(1)} %bitcast.121, f32[10]{0:T(128)} %param.17, ...), kind=kOutput, calls=%fused_computation.37 | convolution fusion | flops 506920960 | bytes 2641960 | tf_op jit(solution)/shard_map/while/body/eval_jaxpr/hts,shp->thp/dot_general | solution.py:73
  338.6 65.9 %all-reduce.4.cloned.1.call-done = (f32[256,128]{1,0:T(8,128)}, f32[256,128]{1,0:T(8,128)}) async-done(((f32[256,128]{1,0:T(8,128)}, f32[256,128]{1,0:T(8,128)}), (f32[256,128]{1,0:T(8,128)}, f32[256,128]{1,0:T(8,128)})) %all-reduce.4.cloned.1.call-update) | async-done | bytes 262160 | tf_op jit(solution)/shard_map/psum | solution.py:148
  404.6 1.6 copy.66
  406.1 1.6 copy.67
  (189 shorter events, 112.7 us)
Async XLA Ops:
  7.2 12.0 %copy-start = (f32[256,128]{1,0:T(8,128)S(1)}, f32[256,128]{1,0:T(8,128)}, u32[]{:S(2)}) copy-start(f32[256,128]{1,0:T(8,128)} %param.14) | copy-start | bytes 393220
  7.2 11.6 %copy-start.2 = (f32[256,640]{1,0:T(8,128)S(1)}, f32[256,640]{1,0:T(8,128)}, u32[]{:S(2)}) copy-start(f32[256,640]{1,0:T(8,128)} %param.19) | copy-start | bytes 1966084
  7.2 140.6 %all-gather.6.cloned.1.call-start = ((), (), s32[]{:S(2)}) async-start(), calls=%async_computation | async-start | bytes 21299200 | tf_op jit(solution)/shard_map/all_gather | solution.py:17
  14.0 130.7 %copy-start.8 = (f32[2,8,2,128]{3,1,2,0:T(8,128)}, f32[2,8,2,128]{3,1,2,0:T(8,128)S(1)}, u32[]{:S(2)}) copy-start(f32[2,8,2,128]{3,1,2,0:T(8,128)S(1)} %copy.44) | copy-start | bytes 49156
  16.4 4.3 %copy-start.11 = (u32[256]{0:T(256)S(1)}, u32[256]{0:T(256)}, u32[]{:S(2)}) copy-start(u32[256]{0:T(256)} %constant.132) | copy-start | bytes 3076
  18.8 121.7 %copy-start.1 = (f32[256,128]{1,0:T(8,128)S(1)}, f32[256,128]{1,0:T(8,128)}, u32[]{:S(2)}) copy-start(f32[256,128]{1,0:T(8,128)} %param.13) | copy-start | bytes 393220
  18.8 222.5 %all-gather.8.cloned.1.call-start = ((), (), s32[]{:S(2)}) async-start(), calls=%async_computation.1 | async-start | bytes 21299200 | tf_op jit(solution)/shard_map/all_gather | solution.py:17
  19.1 122.5 %copy-start.7 = (f32[10,256]{1,0:T(8,128)S(1)}, f32[10,256]{1,0:T(8,128)}, u32[]{:S(2)}) copy-start(f32[10,256]{1,0:T(8,128)} %param.15) | copy-start | bytes 30724
  19.1 122.5 %copy-start.10 = (f32[10]{0:T(128)S(1)}, f32[10]{0:T(128)}, u32[]{:S(2)}) copy-start(f32[10]{0:T(128)} %param.17) | copy-start | bytes 124
  20.6 384.0 %all-reduce.4.cloned.1.call-start = ((), (), s32[]{:S(2)}) async-start(), calls=%async_computation.2 | async-start | bytes 524288 | tf_op jit(solution)/shard_map/psum | solution.py:148
  140.5 4.3 %copy-start.9 = (pred[256,256]{1,0:T(8,128)(4,1)}, pred[256,256]{1,0:T(8,128)(4,1)S(1)}, u32[]{:S(2)}) copy-start(pred[256,256]{1,0:T(8,128)(4,1)S(1)} %fusion.62) | copy-start | bytes 196612
  140.9 3.2 copy-start.6
  326.7 3.5 copy-start.4
  326.7 5.7 %copy-start.3 = (f32[256,128]{1,0:T(8,128)S(1)}, f32[256,128]{1,0:T(8,128)}, u32[]{:S(2)}) copy-start(f32[256,128]{1,0:T(8,128)} %convolution_bitcast_fusion.5) | copy-start | bytes 393220
  326.7 5.7 %copy-start.5 = (f32[256,128]{1,0:T(8,128)S(1)}, f32[256,128]{1,0:T(8,128)}, u32[]{:S(2)}) copy-start(f32[256,128]{1,0:T(8,128)} %convolution_bitcast_fusion.4) | copy-start | bytes 393220
Sparse Core Ops, SparseCore 0:
  18.9 112.2 all-gather.5
  134.5 106.7 all-gather.7
  333.5 70.9 all-reduce.3
where the time goes:
time: 419 us; the launch traced here: 414 us
  waiting for transfers between devices  127 us (30%)
  blocking collectives  114 us (27%)
  other arithmetic  73.7 us (18%)
  local copies, waits for them, and re-layouts  53.9 us (13%)
  matrix products  28.2 us (7%)
  between operations  15.4 us (4%)
    unnamed x1, blocking collectives  114 us
    add x63, other arithmetic, combine_pair(): later_part[0][:, None, None] * earlier[1] + later_part[1]  68.3 us
    psum x1, waiting for transfers between devices, body(): grad_b, grad_c = lax.psum((grad_b, grad_c), 'head')  65.9 us
    all_gather x2, waiting for transfers between devices, entering_2(): gathered = jax.tree.map(lambda a: lax.all_gather(a, axis), part)  61 us
    mul x63, local copies, waits for them, and re-layouts, combine_pair(): later_part[0][:, None, None] * earlier[1] + later_part[1]  43.9 us
  transfers between devices with their start and end apart: 3, of which 2 were waited for; matrix products, arithmetic and copies ran while one was open for 12% of the time, Pallas kernels for 0%

commit v1 on v0

v1 whole, which is shorter than its diff:
```python
import functools

import jax
import jax.numpy as jnp
from jax import lax
from jax.experimental import pallas as pl
from jax.experimental.pallas import tpu as pltpu
from jax.sharding import PartitionSpec as P

HEAD_SIZE = 64
STATE = 128
F32 = jnp.float32
BF16 = jnp.bfloat16
INTERPRET = False

NN = (((1,), (0,)), ((), ()))
NT = (((1,), (1,)), ((), ()))
TN = (((0,), (0,)), ((), ()))


def exact(a, b, dims):
    return lax.dot_general(
        a, b, dims, precision=lax.Precision.HIGHEST, preferred_element_type=F32
    )


def halves(a):
    high = a.astype(BF16)
    return high, (a - high.astype(F32)).astype(BF16)


def dot3(a, b, dims):
    (ah, al), (bh, bl) = a, b
    one = functools.partial(lax.dot_general, dimension_numbers=dims, preferred_element_type=F32)
    return one(ah, bh) + (one(ah, bl) + one(al, bh))


def lanes_of(cols, pair, rows):
    lane = lax.broadcasted_iota(jnp.int32, (rows, 128), 1)
    left = jnp.broadcast_to(cols[:, 2 * pair : 2 * pair + 1], (rows, 128))
    right = jnp.broadcast_to(cols[:, 2 * pair + 1 : 2 * pair + 2], (rows, 128))
    return jnp.where(lane < HEAD_SIZE, left, right)


def call(kernel, outs, args, scalars=0, flops=0, name=None):
    specs = [pl.BlockSpec(memory_space=pltpu.SMEM)] * scalars
    specs += [pl.BlockSpec(memory_space=pltpu.VMEM)] * (len(args) - scalars)
    moved = sum(a.size * a.dtype.itemsize for a in list(args) + list(outs))
    return pl.pallas_call(
        kernel,
        out_shape=tuple(outs),
        in_specs=specs,
        out_specs=tuple(pl.BlockSpec(memory_space=pltpu.VMEM) for _ in outs),
        cost_estimate=pl.CostEstimate(flops=flops, bytes_accessed=moved, transcendentals=0),
        interpret=INTERPRET,
        name=name,
    )(*args)


def prepare(
    place, rates, lens, steps, x, g, bmat, cmat, pack, xs_ref, ge_ref, er_ref, de_ref, mask, row, end
):
    heads, length = steps.shape
    docs = lens.shape[1]
    first = place[0].astype(F32)
    lengths = jnp.broadcast_to(lens[...].astype(F32), (8, docs))
    up = lax.broadcasted_iota(jnp.int32, (docs, docs), 0)
    across = lax.broadcasted_iota(jnp.int32, (docs, docs), 1)
    start_row = exact(lengths, (up < across).astype(F32), NN)[0:1, :]
    start_col = exact((across < up).astype(F32), lengths, NT)[:, 0:1]
    at_col = first + lax.broadcasted_iota(jnp.int32, (length, docs), 0).astype(F32)
    at_row = first + lax.broadcasted_iota(jnp.int32, (docs, length), 1).astype(F32)
    doc_col = jnp.sum((start_row <= at_col).astype(F32), axis=1, keepdims=True)
    doc_row = jnp.sum((start_col <= at_row).astype(F32), axis=0, keepdims=True)
    before = jnp.sum((start_row < first).astype(F32), axis=1, keepdims=True)
    last = jnp.sum((start_row <= first + (length - 1)).astype(F32), axis=1, keepdims=True)
    inside = (doc_col == before).astype(F32)
    onward = (doc_col == last).astype(F32)

    head_at = lax.broadcasted_iota(jnp.int32, (heads, length), 0)
    rate = jnp.zeros((heads, length), F32)
    for h in range(heads):
        rate = jnp.where(head_at == h, rates[h], rate)
    dt = steps[...]
    log_decay = -rate * dt
    t_at = lax.broadcasted_iota(jnp.int32, (length, length), 0)
    s_at = lax.broadcasted_iota(jnp.int32, (length, length), 1)
    running = exact((s_at <= t_at).astype(F32), log_decay, NT)
    dt_col = exact((s_at == t_at).astype(F32), dt, NT)
    er = jnp.exp(running)
    de = dt_col * jnp.exp(-running)
    er_ref[...] = er
    de_ref[...] = de
    ended = jnp.exp(jnp.broadcast_to(jnp.sum(log_decay, axis=1, keepdims=True), (heads, 128)))
    end[...] = ended
    whole = ended * (before == last).astype(F32)

    lane = lax.broadcasted_iota(jnp.int32, (length, 128), 1)
    mask[...] = jnp.where(lane == 0, inside, jnp.where(lane == 1, onward, doc_col))
    row[...] = jnp.broadcast_to(doc_row, (8, length))

    b_out = halves(bmat[...] * onward)
    c_in = halves(cmat[...] * inside)
    for j in range(heads // 2):
        part = slice(128 * j, 128 * j + 128)
        scaled = x[:, part] * lanes_of(de, j, length)
        xs_ref[:, part] = scaled
        state = dot3(halves(scaled), b_out, TN)
        grown = g[:, part] * lanes_of(er, j, length)
        ge_ref[:, part] = grown
        grad = dot3(halves(grown), c_in, TN)
        for k in range(2):
            h, rows = 2 * j + k, slice(64 * k, 64 * k + 64)
            pack[h, 0:64, :] = state[rows, :] * ended[h : h + 1, :]
            pack[h, 64:128, :] = grad[rows, :]
            pack[h, 128:136, :] = jnp.broadcast_to(whole[h : h + 1, :], (8, 128))


def chip_states(place, mine, other, fwd, bwd, decay):
    core = place[1]
    half = fwd.shape[0]
    for k in range(half):
        h = core * half + k
        a, b = mine[h], other[h]
        early = jnp.where(core == 0, a, b)
        late = jnp.where(core == 0, b, a)
        d_early, d_late = early[128:129, :], late[128:129, :]
        fwd[k] = late[0:64, :] + d_late * early[0:64, :]
        bwd[k] = early[64:128, :] + d_early * late[64:128, :]
        decay[k] = jnp.broadcast_to(d_early * d_late, (8, 128))


def two_chips(fwd, bwd, decay, fwd_in, bwd_in, fwd_out, bwd_out):
    for k in range(fwd.shape[0]):
        d = decay[k][0:1, :]
        fwd_out[k] = fwd[k] + d * fwd_in[k]
        bwd_out[k] = bwd[k] + d * bwd_in[k]


def local(bmat, cmat, xs, ge, mask, row, y0, gx0, gb0, gc0):
    length = bmat.shape[0]
    t_at = lax.broadcasted_iota(jnp.int32, (length, length), 0)
    s_at = lax.broadcasted_iota(jnp.int32, (length, length), 1)
    seen = (mask[:, 2:3] == row[0:1, :]) & (s_at <= t_at)
    b2, c2, x2, g2 = halves(bmat[...]), halves(cmat[...]), halves(xs[...]), halves(ge[...])
    scores = halves(jnp.where(seen, dot3(c2, b2, NT), 0.0))
    y0[...] = dot3(scores, x2, NN)
    gx0[...] = dot3(scores, g2, TN)
    weight = halves(jnp.where(seen, dot3(g2, x2, NT), 0.0))
    gb0[...] = dot3(weight, c2, TN)
    gc0[...] = dot3(weight, b2, NN)


def finish_maps(
    place, other, f_own, f_far, b_own, b_far, end, xs, ge, mask, gb0, gc0, gb, gc, s_ref, a_ref
):
    core = place[1]
    heads = other.shape[0]
    half = heads // 2
    for h in range(heads):
        own = core == h // half
        k = h % half
        fwd = jnp.where(own, f_own[k], f_far[k])
        bwd = jnp.where(own, b_own[k], b_far[k])
        d = other[h, 128:129, :]
        state = jnp.where(core == 1, other[h, 0:64, :] + d * fwd, fwd)
        after = jnp.where(core == 0, other[h, 64:128, :] + d * bwd, bwd)
        s_ref[64 * h : 64 * h + 64, :] = state
        a_ref[64 * h : 64 * h + 64, :] = after * end[h : h + 1, :]
    state, after = halves(s_ref[...]), halves(a_ref[...])
    gc[...] = gc0[...] + mask[:, 0:1] * dot3(halves(ge[...]), state, NN)
    gb[...] = gb0[...] + mask[:, 1:2] * dot3(halves(xs[...]), after, NN)


def finish_values(skips, x, g, bmat, cmat, er, de, mask, s_ref, a_ref, y0, gx0, y, gx):
    length = bmat.shape[0]
    c_in = halves(cmat[...] * mask[:, 0:1])
    b_out = halves(bmat[...] * mask[:, 1:2])
    er_cols, de_cols = er[...], de[...]
    lane = lax.broadcasted_iota(jnp.int32, (1, 128), 1)
    for j in range(x.shape[1] // 128):
        part = slice(128 * j, 128 * j + 128)
        skip = jnp.where(lane < HEAD_SIZE, skips[2 * j], skips[2 * j + 1])
        far = dot3(c_in, halves(s_ref[part, :]), NT)
        y[:, part] = (
            lanes_of(er_cols, j, length) * (y0[:, part] + far) + skip * x[:, part]
        ).astype(BF16)
        far = dot3(b_out, halves(a_ref[part, :]), NT)
        gx[:, part] = (
            lanes_of(de_cols, j, length) * (gx0[:, part] + far) + skip * g[:, part]
        ).astype(BF16)


def body(values, input_map, output_map, step_sizes, decay_rates, skip_gains, doc_lengths, out_grad):
    length, width = values.shape
    heads = width // HEAD_SIZE
    half = heads // 2
    shape = jax.ShapeDtypeStruct
    index = lax.axis_index("seq")
    place = jnp.stack([index * length, index % 2]).astype(jnp.int32)
    count = lax.axis_size("seq")
    swap = [(i, i ^ 1) for i in range(count)]
    ahead = [(i, i + 2) for i in range(count - 2)]
    back = [(i + 2, i) for i in range(count - 2)]

    pack, xs, ge, er, de, mask, row, end = call(
        prepare,
        [
            shape((heads, 136, STATE), F32),
            shape((length, width), F32),
            shape((length, width), F32),
            shape((length, heads), F32),
            shape((length, heads), F32),
            shape((length, 128), F32),
            shape((8, length), F32),
            shape((heads, 128), F32),
        ],
        (
            place,
            decay_rates,
            doc_lengths.reshape(1, -1),
            step_sizes,
            values,
            out_grad,
            input_map,
            output_map,
        ),
        scalars=2,
        flops=12 * length * width * STATE,
        name="prepare",
    )
    other = lax.ppermute(pack, "seq", swap)
    y0, gx0, gb0, gc0 = call(
        local,
        [
            shape((length, width), F32),
            shape((length, width), F32),
            shape((length, STATE), F32),
            shape((length, STATE), F32),
        ],
        (input_map, output_map, xs, ge, mask, row),
        flops=18 * length * width * length,
        name="local",
    )
    states = shape((half, HEAD_SIZE, STATE), F32)
    fwd, bwd, decay = call(
        chip_states,
        [states, states, shape((half, 8, STATE), F32)],
        (place, pack, other),
        scalars=1,
        name="chip_states",
    )
    fwd_in = lax.ppermute(fwd, "seq", ahead)
    bwd_in = lax.ppermute(bwd, "seq", back)
    fwd, bwd = call(two_chips, [states, states], (fwd, bwd, decay, fwd_in, bwd_in), name="two_chips")
    f_own = lax.ppermute(fwd, "seq", ahead)
    b_own = lax.ppermute(bwd, "seq", back)
    f_far = lax.ppermute(f_own, "seq", swap)
    b_far = lax.ppermute(b_own, "seq", swap)
    gb, gc, state, after = call(
        finish_maps,
        [
            shape((length, STATE), F32),
            shape((length, STATE), F32),
            shape((width, STATE), F32),
            shape((width, STATE), F32),
        ],
        (place, other, f_own, f_far, b_own, b_far, end, xs, ge, mask, gb0, gc0),
        scalars=1,
        flops=12 * length * width * STATE,
        name="finish_maps",
    )
    near = [(0, 1), (1, 0), (2, 3), (3, 2)]
    cross = [(0, 3), (3, 0), (1, 2), (2, 1)]
    gb = gb + lax.ppermute(gb, "head", near)
    gc = gc + lax.ppermute(gc, "head", cross)
    y, gx = call(
        finish_values,
        [shape((length, width), BF16), shape((length, width), BF16)],
        (
            skip_gains,
            values,
            out_grad,
            input_map,
            output_map,
            er,
            de,
            mask,
            state,
            after,
            y0,
            gx0,
        ),
        scalars=1,
        flops=12 * length * width * STATE,
        name="finish_values",
    )
    gb = gb + lax.ppermute(gb, "head", cross)
    gc = gc + lax.ppermute(gc, "head", near)
    return y, gx, gb, gc


def solution(mesh):
    placed = (
        P("seq", "head"),
        P("seq", None),
        P("seq", None),
        P("head", "seq"),
        P("head"),
        P("head"),
        P(),
        P("seq", "head"),
    )
    return jax.shard_map(
        body,
        mesh=mesh,
        in_specs=placed,
        out_specs=(P("seq", "head"), P("seq", "head"), P("seq", None), P("seq", None)),
        check_vma=False,
    )
```

time: 419 us -> 63.9 us (0.15)
  waiting for transfers between devices: 127 us -> 12.3 us
  blocking collectives: 114 us -> 0 us
  other arithmetic: 73.7 us -> 2.86 us
  local copies, waits for them, and re-layouts: 53.9 us -> 2.23 us
  matrix products: 28.2 us -> 0 us
  starting transfers between devices: 0.12 us -> 25.1 us
  Pallas kernels: 0 us -> 19.9 us
  between operations: 15.4 us -> 0.74 us
    unnamed x1 -> x0, blocking collectives: 114 us -> none
    add x64 -> x4, other arithmetic: 68.3 us -> 2.28 us  [the longest x1 0.92 us: body(): gb = gb + lax.ppermute(gb, 'head', near)]
    psum x1 -> x0, waiting for transfers between devices: 65.9 us -> none  [body(): grad_b, grad_c = lax.psum((grad_b, grad_c), 'head')]
    all_gather x2 -> x0, waiting for transfers between devices: 61 us -> none  [entering_2(): gathered = jax.tree.map(lambda a: lax.all_gather(a, axis), part)]
    mul x63 -> x0, local copies, waits for them, and re-layouts: 43.9 us -> none  [combine_pair(): later_part[0][:, None, None] * earlier[1] + later_part[1]]
    dot_general x16 -> x0, matrix products: 28.2 us -> none  [the longest x1 4.28 us: forward(): result = jnp.einsum('hts,shp->thp', mixing, scaled, precision=highest)]
    ppermute x0 -> x11, starting transfers between devices: none -> 25.1 us  [the longest x1 6.13 us: body(): b_own = lax.ppermute(bwd, 'seq', back)]
    pallas_call x0 -> x6, Pallas kernels: none -> 19.9 us  [call(): pl.pallas_call(kernel, out_shape=tuple(outs), in_specs=specs, out_specs=t...]
  transfers between devices with their start and end apart: 3 -> 11, of which waited for: 2 -> 7; matrix products, arithmetic and copies ran while one was open for 12% -> 3% of each run, Pallas kernels for 0% -> 13%
where the time goes in v1:
time: 63.9 us; the launch traced here: 63.2 us
  starting transfers between devices  25.1 us (39%)
  Pallas kernels  19.9 us (31%)
  waiting for transfers between devices  12.3 us (19%)
  other arithmetic  2.86 us (4%)
  local copies, waits for them, and re-layouts  2.23 us (3%)
  between operations  0.74 us (1%)
    pallas_call x6, Pallas kernels, call(): pl.pallas_call(kernel, out_shape=tuple(outs), in_specs=specs, out_specs=t...  19.9 us
    ppermute x1, starting transfers between devices, body(): b_own = lax.ppermute(bwd, 'seq', back)  6.13 us
    ppermute x1, starting transfers between devices, body(): bwd_in = lax.ppermute(bwd, 'seq', back)  5.83 us
    ppermute x1, starting transfers between devices, body(): fwd_in = lax.ppermute(fwd, 'seq', ahead)  3.81 us
    ppermute x1, starting transfers between devices, body(): gb = gb + lax.ppermute(gb, 'head', cross)  3.1 us
    ppermute x1, waiting for transfers between devices, body(): fwd_in = lax.ppermute(fwd, 'seq', ahead)  2.77 us
    ppermute x1, waiting for transfers between devices, body(): other = lax.ppermute(pack, 'seq', swap)  2.35 us
    ppermute x1, waiting for transfers between devices, body(): gb = gb + lax.ppermute(gb, 'head', near)  2.3 us
  transfers between devices with their start and end apart: 11, of which 7 were waited for; matrix products, arithmetic and copies ran while one was open for 3% of the time, Pallas kernels for 13%

profile of v1, /device:TPU:2, one launch (start us, length us, event | category | flops | bytes accessed | tf_op | source)
XLA Modules:
  0.0 63.2 jit_solution(308493130250785783)
XLA Ops:
  0.6 0.6 pad_add_fusion.place
  1.2 4.6 %prepare.1 = (f32[10,136,128]{2,1,0:T(8,128)}, f32[256,640]{1,0:T(8,128)}, f32[256,640]{1,0:T(8,128)}, f32[256,10]{1,0:T(8,128)}, f32[256,10]{1,0:T(8,128)}, /*i...) custom-call(s32[2]{0:T(128)} %pad_add_fusion.place, f32[10]{0:T(128)} %rates.1, s32[1,128]{1,0:T(1,128)} %bitcast.3, ...), custom_call_target="tpu_custom_call" | custom-call | flops 251658240 | bytes 3755568 | tf_op jit(solution)/shard_map/prepare/pallas_call | solution.py:49
  5.8 0.1 collective-permute-start
  5.9 2.4 %collective-permute-done.other = f32[10,136,128]{2,1,0:T(8,128)S(1)} collective-permute-done((f32[10,136,128]{2,1,0:T(8,128)}, f32[10,136,128]{2,1,0:T(8,128)S(1)}, u32[]{:S(2)}, u32[]{:S(2)}) %collective-permute-start) | collective-permute-done | bytes 696352 | tf_op jit(solution)/shard_map/ppermute | solution.py:232
  8.2 0.8 %copy-done = f32[10,136,128]{2,1,0:T(8,128)} copy-done((f32[10,136,128]{2,1,0:T(8,128)}, f32[10,136,128]{2,1,0:T(8,128)S(1)}, u32[]{:S(2)}) %copy-start) | copy-done | bytes 696344
  9.1 2.1 %chip_states.1 = (f32[5,64,128]{2,1,0:T(8,128)}, f32[5,64,128]{2,1,0:T(8,128)}, f32[5,8,128]{2,1,0:T(8,128)}) custom-call(s32[2]{0:T(128)} %pad_add_fusion.place, f32[10,136,128]{2,1,0:T(8,128)} %get-tuple-element.30.mine, f32[10,136,128]{2,1,0:T(8,128)} %copy-done), custom_call_target="tpu_custom_call" | custom-call | bytes 1740808 | tf_op jit(solution)/shard_map/chip_states/pallas_call | solution.py:49
  11.2 3.8 %collective-permute-start.1 = (f32[5,64,128]{2,1,0:T(8,128)}, f32[5,64,128]{2,1,0:T(8,128)S(1)}, u32[]{:S(2)}, u32[]{:S(2)}) collective-permute-start(f32[5,64,128]{2,1,0:T(8,128)} %get-tuple-element.31.fwd), channel_id=1, source_target_pairs={{0,8},{4,12},{8,16},{12,20},{16,24},{20,28},{24,32},{28,36},{32,40... | collective-permute-start | bytes 491528 | tf_op jit(solution)/shard_map/ppermute | solution.py:253
  15.0 5.8 %collective-permute-start.2 = (f32[5,64,128]{2,1,0:T(8,128)}, f32[5,64,128]{2,1,0:T(8,128)S(1)}, u32[]{:S(2)}, u32[]{:S(2)}) collective-permute-start(f32[5,64,128]{2,1,0:T(8,128)} %get-tuple-element.32.bwd), channel_id=1, source_target_pairs={{8,0},{12,4},{16,8},{20,12},{24,16},{28,20},{32,24},{36,28},{40,32... | collective-permute-start | bytes 491528 | tf_op jit(solution)/shard_map/ppermute | solution.py:254
  20.8 2.8 %collective-permute-done.1.fwd_in = f32[5,64,128]{2,1,0:T(8,128)S(1)} collective-permute-done((f32[5,64,128]{2,1,0:T(8,128)}, f32[5,64,128]{2,1,0:T(8,128)S(1)}, u32[]{:S(2)}, u32[]{:S(2)}) %collective-permute-start.1) | collective-permute-done | bytes 163872 | tf_op jit(solution)/shard_map/ppermute | solution.py:253
  23.6 1.3 %collective-permute-done.2.bwd_in = f32[5,64,128]{2,1,0:T(8,128)S(1)} collective-permute-done((f32[5,64,128]{2,1,0:T(8,128)}, f32[5,64,128]{2,1,0:T(8,128)S(1)}, u32[]{:S(2)}, u32[]{:S(2)}) %collective-permute-start.2) | collective-permute-done | bytes 163872 | tf_op jit(solution)/shard_map/ppermute | solution.py:254
  24.9 0.7 %copy-done.6 = f32[5,64,128]{2,1,0:T(8,128)} copy-done((f32[5,64,128]{2,1,0:T(8,128)}, f32[5,64,128]{2,1,0:T(8,128)S(1)}, u32[]{:S(2)}) %copy-start.6) | copy-done | bytes 163864
  25.5 1.9 %two_chips.1 = (f32[5,64,128]{2,1,0:T(8,128)}, f32[5,64,128]{2,1,0:T(8,128)}) custom-call(f32[5,64,128]{2,1,0:T(8,128)} %get-tuple-element.31.fwd, f32[5,64,128]{2,1,0:T(8,128)} %get-tuple-element.32.bwd, f32[5,8,128]{2,1,0:T(8,128)} %get-tuple-element.33.decay, f32[5,64,128]{2,1,0:T(8,128)} %copy-done.5, f32[5,64,128]{2,1,0:T(8,128)} %copy-done.6), custom_call_target="tpu_custom_call" | custom-call | bytes 1003520 | tf_op jit(solution)/shard_map/two_chips/pallas_call | solution.py:49
  27.5 2.2 %collective-permute-start.3 = (f32[5,64,128]{2,1,0:T(8,128)}, f32[5,64,128]{2,1,0:T(8,128)S(1)}, u32[]{:S(2)}, u32[]{:S(2)}) collective-permute-start(f32[5,64,128]{2,1,0:T(8,128)} %get-tuple-element.34), channel_id=1, source_target_pairs={{0,8},{4,12},{8,16},{12,20},{16,24},{20,28},{24,32},{28,36},{32,40... | collective-permute-start | bytes 491528 | tf_op jit(solution)/shard_map/ppermute | solution.py:256
  29.7 6.1 %collective-permute-start.5 = (f32[5,64,128]{2,1,0:T(8,128)}, f32[5,64,128]{2,1,0:T(8,128)S(1)}, u32[]{:S(2)}, u32[]{:S(2)}) collective-permute-start(f32[5,64,128]{2,1,0:T(8,128)} %get-tuple-element.35), channel_id=1, source_target_pairs={{8,0},{12,4},{16,8},{20,12},{24,16},{28,20},{32,24},{36,28},{40,32... | collective-permute-start | bytes 491528 | tf_op jit(solution)/shard_map/ppermute | solution.py:257
  35.8 1.9 %collective-permute-done.3.f_own = f32[5,64,128]{2,1,0:T(8,128)S(1)} collective-permute-done((f32[5,64,128]{2,1,0:T(8,128)}, f32[5,64,128]{2,1,0:T(8,128)S(1)}, u32[]{:S(2)}, u32[]{:S(2)}) %collective-permute-start.3) | collective-permute-done | bytes 163872 | tf_op jit(solution)/shard_map/ppermute | solution.py:256
  37.7 0.0 collective-permute-start.4
  37.7 1.3 %collective-permute-done.5.b_own = f32[5,64,128]{2,1,0:T(8,128)S(1)} collective-permute-done((f32[5,64,128]{2,1,0:T(8,128)}, f32[5,64,128]{2,1,0:T(8,128)S(1)}, u32[]{:S(2)}, u32[]{:S(2)}) %collective-permute-start.5) | collective-permute-done | bytes 163872 | tf_op jit(solution)/shard_map/ppermute | solution.py:257
  39.0 4.3 %local.1 = (f32[256,640]{1,0:T(8,128)}, f32[256,640]{1,0:T(8,128)}, f32[256,128]{1,0:T(8,128)}, f32[256,128]{1,0:T(8,128)}) custom-call(f32[256,128]{1,0:T(8,128)} %bmat.5, f32[256,128]{1,0:T(8,128)} %cmat.5, f32[256,640]{1,0:T(8,128)} %get-tuple-element.37.xs, f32[256,640]{1,0:T(8,128)} %get-tuple-element.38.ge, f32[256,128]{1,0:T(8,128)} %get-tuple-element.29.mask, ...), custom_call_target="tpu_custom_call" | custom-call | flops 754974720 | bytes 3284992 | tf_op jit(solution)/shard_map/local/pallas_call | solution.py:49
  43.4 0.0 copy-start.3
  43.4 0.6 %copy-done.3 = f32[5,64,128]{2,1,0:T(8,128)} copy-done((f32[5,64,128]{2,1,0:T(8,128)}, f32[5,64,128]{2,1,0:T(8,128)S(1)}, u32[]{:S(2)}) %copy-start.3) | copy-done | bytes 163864
  44.0 0.1 copy-done.4
  44.1 3.2 %finish_maps.1 = (f32[256,128]{1,0:T(8,128)}, f32[256,128]{1,0:T(8,128)}, f32[640,128]{1,0:T(8,128)}, f32[640,128]{1,0:T(8,128)}) custom-call(s32[2]{0:T(128)} %pad_add_fusion.place, f32[10,136,128]{2,1,0:T(8,128)} %copy-done, f32[5,64,128]{2,1,0:T(8,128)} %copy-done.1, f32[5,64,128]{2,1,0:T(8,128)} %copy-done.3, f32[5,64,128]{2,1,0:T(8,128)} %copy-done.2, ...), custom_call_target="tpu_custom_call" | custom-call | flops 251658240 | bytes 3978248 | tf_op jit(solution)/shard_map/finish_maps/pallas_call | solution.py:49
  47.4 1.6 %collective-permute-start.7 = (f32[256,128]{1,0:T(8,128)}, f32[256,128]{1,0:T(8,128)S(1)}, u32[]{:S(2)}, u32[]{:S(2)}) collective-permute-start(f32[256,128]{1,0:T(8,128)} %get-tuple-element.48), channel_id=1, source_target_pairs={{0,1},{1,0},{2,3},{3,2},{4,5},{5,4},{6,7},{7,6},{8,9},{9,8},{10,11... | collective-permute-start | bytes 393224 | tf_op jit(solution)/shard_map/ppermute | solution.py:275
  48.9 2.2 %collective-permute-start.9 = (f32[256,128]{1,0:T(8,128)}, f32[256,128]{1,0:T(8,128)S(1)}, u32[]{:S(2)}, u32[]{:S(2)}) collective-permute-start(f32[256,128]{1,0:T(8,128)} %get-tuple-element.49), channel_id=1, source_target_pairs={{0,3},{3,0},{1,2},{2,1},{4,7},{7,4},{5,6},{6,5},{8,11},{11,8},{9,1... | collective-permute-start | bytes 393224 | tf_op jit(solution)/shard_map/ppermute | solution.py:276
  51.1 2.3 %collective-permute-done.7 = f32[256,128]{1,0:T(8,128)S(1)} collective-permute-done((f32[256,128]{1,0:T(8,128)}, f32[256,128]{1,0:T(8,128)S(1)}, u32[]{:S(2)}, u32[]{:S(2)}) %collective-permute-start.7) | collective-permute-done | bytes 131104 | tf_op jit(solution)/shard_map/ppermute | solution.py:275
  53.4 0.9 %add.17 = f32[256,128]{1,0:T(8,128)S(1)} add(f32[256,128]{1,0:T(8,128)} %get-tuple-element.48, f32[256,128]{1,0:T(8,128)S(1)} %collective-permute-done.7) | non-fusion elementwise | flops 32768 | bytes 393216 | tf_op jit(solution)/shard_map/add | solution.py:275
  54.3 3.1 %collective-permute-start.8 = (f32[256,128]{1,0:T(8,128)S(1)}, f32[256,128]{1,0:T(8,128)S(1)}, u32[]{:S(2)}, u32[]{:S(2)}) collective-permute-start(f32[256,128]{1,0:T(8,128)S(1)} %add.17), channel_id=1, source_target_pairs={{0,3},{3,0},{1,2},{2,1},{4,7},{7,4},{5,6},{6,5},{8,11},{11,8},{9,1... | collective-permute-start | bytes 393224 | tf_op jit(solution)/shard_map/ppermute | solution.py:298
  57.5 0.2 collective-permute-start.10
  57.7 3.8 %finish_values.1 = (bf16[256,640]{1,0:T(8,128)(2,1)}, bf16[256,640]{1,0:T(8,128)(2,1)}) custom-call(f32[10]{0:T(128)} %skips.1, f32[256,640]{1,0:T(8,128)} %x.3, f32[256,640]{1,0:T(8,128)} %g.3, f32[256,128]{1,0:T(8,128)} %bmat.5, f32[256,128]{1,0:T(8,128)} %cmat.5, f32[256,10]{1,0:T(8,128)} %get-tuple-element.27.er, f32[256,10]{1,0:T(8,128)} %get-tuple-element.28.de, ...), custom_call_target="tpu_custom_call" | custom-call | flops 251658240 | bytes 4345896 | tf_op jit(solution)/shard_map/finish_values/pallas_call | solution.py:49
  61.5 0.7 %add.18 = f32[256,128]{1,0:T(8,128)} add(f32[256,128]{1,0:T(8,128)S(1)} %add.17, f32[256,128]{1,0:T(8,128)S(1)} %collective-permute-done.8) | non-fusion elementwise | flops 32768 | bytes 393216 | tf_op jit(solution)/shard_map/add | solution.py:298
  62.2 0.4 collective-permute-done.10
  62.5 0.7 %add.20 = f32[256,128]{1,0:T(8,128)} add(f32[256,128]{1,0:T(8,128)S(1)} %add.19, f32[256,128]{1,0:T(8,128)S(1)} %collective-permute-done.10) | non-fusion elementwise | flops 32768 | bytes 393216 | tf_op jit(solution)/shard_map/add | solution.py:299
  (17 shorter events, 0.0 us)
Async XLA Ops:
  5.8 2.5 %collective-permute-start = (f32[10,136,128]{2,1,0:T(8,128)}, f32[10,136,128]{2,1,0:T(8,128)S(1)}, u32[]{:S(2)}, u32[]{:S(2)}) collective-permute-start(f32[10,136,128]{2,1,0:T(8,128)} %get-tuple-element.30.mine), channel_id=1, source_target_pairs={{0,4},{4,0},{8,12},{12,8},{16,20},{20,16},{24,28},{28,24},{32,36},... | collective-permute-start | bytes 2088968 | tf_op jit(solution)/shard_map/ppermute | solution.py:232
  8.2 0.9 %copy-start = (f32[10,136,128]{2,1,0:T(8,128)}, f32[10,136,128]{2,1,0:T(8,128)S(1)}, u32[]{:S(2)}) copy-start(f32[10,136,128]{2,1,0:T(8,128)S(1)} %collective-permute-done.other) | copy-start | bytes 2088964
  11.2 12.4 %collective-permute-start.1 = (f32[5,64,128]{2,1,0:T(8,128)}, f32[5,64,128]{2,1,0:T(8,128)S(1)}, u32[]{:S(2)}, u32[]{:S(2)}) collective-permute-start(f32[5,64,128]{2,1,0:T(8,128)} %get-tuple-element.31.fwd), channel_id=1, source_target_pairs={{0,8},{4,12},{8,16},{12,20},{16,24},{20,28},{24,32},{28,36},{32,40... | collective-permute-start | bytes 491528 | tf_op jit(solution)/shard_map/ppermute | solution.py:253
  15.0 9.9 %collective-permute-start.2 = (f32[5,64,128]{2,1,0:T(8,128)}, f32[5,64,128]{2,1,0:T(8,128)S(1)}, u32[]{:S(2)}, u32[]{:S(2)}) collective-permute-start(f32[5,64,128]{2,1,0:T(8,128)} %get-tuple-element.32.bwd), channel_id=1, source_target_pairs={{8,0},{12,4},{16,8},{20,12},{24,16},{28,20},{32,24},{36,28},{40,32... | collective-permute-start | bytes 491528 | tf_op jit(solution)/shard_map/ppermute | solution.py:254
  23.6 1.3 %copy-start.5 = (f32[5,64,128]{2,1,0:T(8,128)}, f32[5,64,128]{2,1,0:T(8,128)S(1)}, u32[]{:S(2)}) copy-start(f32[5,64,128]{2,1,0:T(8,128)S(1)} %collective-permute-done.1.fwd_in) | copy-start | bytes 491524
  24.9 0.7 %copy-start.6 = (f32[5,64,128]{2,1,0:T(8,128)}, f32[5,64,128]{2,1,0:T(8,128)S(1)}, u32[]{:S(2)}) copy-start(f32[5,64,128]{2,1,0:T(8,128)S(1)} %collective-permute-done.2.bwd_in) | copy-start | bytes 491524
  27.5 10.2 %collective-permute-start.3 = (f32[5,64,128]{2,1,0:T(8,128)}, f32[5,64,128]{2,1,0:T(8,128)S(1)}, u32[]{:S(2)}, u32[]{:S(2)}) collective-permute-start(f32[5,64,128]{2,1,0:T(8,128)} %get-tuple-element.34), channel_id=1, source_target_pairs={{0,8},{4,12},{8,16},{12,20},{16,24},{20,28},{24,32},{28,36},{32,40... | collective-permute-start | bytes 491528 | tf_op jit(solution)/shard_map/ppermute | solution.py:256
  29.7 9.3 %collective-permute-start.5 = (f32[5,64,128]{2,1,0:T(8,128)}, f32[5,64,128]{2,1,0:T(8,128)S(1)}, u32[]{:S(2)}, u32[]{:S(2)}) collective-permute-start(f32[5,64,128]{2,1,0:T(8,128)} %get-tuple-element.35), channel_id=1, source_target_pairs={{8,0},{12,4},{16,8},{20,12},{24,16},{28,20},{32,24},{36,28},{40,32... | collective-permute-start | bytes 491528 | tf_op jit(solution)/shard_map/ppermute | solution.py:257
  37.7 5.6 %copy-start.1 = (f32[5,64,128]{2,1,0:T(8,128)}, f32[5,64,128]{2,1,0:T(8,128)S(1)}, u32[]{:S(2)}) copy-start(f32[5,64,128]{2,1,0:T(8,128)S(1)} %collective-permute-done.3.f_own) | copy-start | bytes 491524
  37.7 5.6 %collective-permute-start.4 = (f32[5,64,128]{2,1,0:T(8,128)S(1)}, f32[5,64,128]{2,1,0:T(8,128)S(1)}, u32[]{:S(2)}, u32[]{:S(2)}) collective-permute-start(f32[5,64,128]{2,1,0:T(8,128)S(1)} %collective-permute-done.3.f_own), channel_id=1, source_target_pairs={{0,4},{4,0},{8,12},{12,8},{16,20},{20,16},{24,28},{28,24},{32,36},... | collective-permute-start | bytes 491528 | tf_op jit(solution)/shard_map/ppermute | solution.py:258
  39.0 4.4 %copy-start.2 = (f32[5,64,128]{2,1,0:T(8,128)}, f32[5,64,128]{2,1,0:T(8,128)S(1)}, u32[]{:S(2)}) copy-start(f32[5,64,128]{2,1,0:T(8,128)S(1)} %collective-permute-done.5.b_own) | copy-start | bytes 491524
  39.0 4.4 %collective-permute-start.6 = (f32[5,64,128]{2,1,0:T(8,128)S(1)}, f32[5,64,128]{2,1,0:T(8,128)S(1)}, u32[]{:S(2)}, u32[]{:S(2)}) collective-permute-start(f32[5,64,128]{2,1,0:T(8,128)S(1)} %collective-permute-done.5.b_own), channel_id=1, source_target_pairs={{0,4},{4,0},{8,12},{12,8},{16,20},{20,16},{24,28},{28,24},{32,36},... | collective-permute-start | bytes 491528 | tf_op jit(solution)/shard_map/ppermute | solution.py:259
  43.4 0.7 %copy-start.3 = (f32[5,64,128]{2,1,0:T(8,128)}, f32[5,64,128]{2,1,0:T(8,128)S(1)}, u32[]{:S(2)}) copy-start(f32[5,64,128]{2,1,0:T(8,128)S(1)} %collective-permute-done.4.f_far) | copy-start | bytes 491524
  43.4 0.7 %copy-start.4 = (f32[5,64,128]{2,1,0:T(8,128)}, f32[5,64,128]{2,1,0:T(8,128)S(1)}, u32[]{:S(2)}) copy-start(f32[5,64,128]{2,1,0:T(8,128)S(1)} %collective-permute-done.6.b_far) | copy-start | bytes 491524
  47.4 6.1 %collective-permute-start.7 = (f32[256,128]{1,0:T(8,128)}, f32[256,128]{1,0:T(8,128)S(1)}, u32[]{:S(2)}, u32[]{:S(2)}) collective-permute-start(f32[256,128]{1,0:T(8,128)} %get-tuple-element.48), channel_id=1, source_target_pairs={{0,1},{1,0},{2,3},{3,2},{4,5},{5,4},{6,7},{7,6},{8,9},{9,8},{10,11... | collective-permute-start | bytes 393224 | tf_op jit(solution)/shard_map/ppermute | solution.py:275
  48.9 8.5 %copy-start.7 = (f32[256,128]{1,0:T(8,128)S(1)}, f32[256,128]{1,0:T(8,128)}, u32[]{:S(2)}) copy-start(f32[256,128]{1,0:T(8,128)} %get-tuple-element.49) | copy-start | bytes 393220
  48.9 8.5 %collective-permute-start.9 = (f32[256,128]{1,0:T(8,128)}, f32[256,128]{1,0:T(8,128)S(1)}, u32[]{:S(2)}, u32[]{:S(2)}) collective-permute-start(f32[256,128]{1,0:T(8,128)} %get-tuple-element.49), channel_id=1, source_target_pairs={{0,3},{3,0},{1,2},{2,1},{4,7},{7,4},{5,6},{6,5},{8,11},{11,8},{9,1... | collective-permute-start | bytes 393224 | tf_op jit(solution)/shard_map/ppermute | solution.py:276
  54.3 7.1 %collective-permute-start.8 = (f32[256,128]{1,0:T(8,128)S(1)}, f32[256,128]{1,0:T(8,128)S(1)}, u32[]{:S(2)}, u32[]{:S(2)}) collective-permute-start(f32[256,128]{1,0:T(8,128)S(1)} %add.17), channel_id=1, source_target_pairs={{0,3},{3,0},{1,2},{2,1},{4,7},{7,4},{5,6},{6,5},{8,11},{11,8},{9,1... | collective-permute-start | bytes 393224 | tf_op jit(solution)/shard_map/ppermute | solution.py:298
  57.5 5.1 %collective-permute-start.10 = (f32[256,128]{1,0:T(8,128)S(1)}, f32[256,128]{1,0:T(8,128)S(1)}, u32[]{:S(2)}, u32[]{:S(2)}) collective-permute-start(f32[256,128]{1,0:T(8,128)S(1)} %add.19), channel_id=1, source_target_pairs={{0,1},{1,0},{2,3},{3,2},{4,5},{5,4},{6,7},{7,6},{8,9},{9,8},{10,11... | collective-permute-start | bytes 393224 | tf_op jit(solution)/shard_map/ppermute | solution.py:299
